TPU v7x, 256 devices: a whole 4x4x8 slice. The times are simulated.
256 devices in a mesh: ev: 256 (over y, z, x, core).
Axes of the slice: x: 4, y: 4, z: 8, core: 2. Of those that a mesh axis runs over, the one named last changes fastest.
Arguments:
- records: bfloat16 [32768, 512], P('ev'), may hold values from -16 to 16
- filter_taps: bfloat16 [65], replicated, may hold values from -0.75 to 0.75
- live_counts: int32 [256], P('ev'), may hold values from 64 to 128, as said below
- pair_valid: int32 [256, 9], P('ev'), may hold values 0 or 1
Outputs:
- correlations: bfloat16 [32768, 10, 25, 128], P('ev')
Inputs may be any that keep to these rules, and one draw needn't show every extreme that they name: The first live_counts[b] events of block b are live and its other rows are padding; some block has all 128 events live.
All inputs are finite; a program needn't handle non-finite values. No bound on the sum of `pair_valid` on one device may be relied on, other than what follows from the above.
Results may differ from a plain program's by a relative error of at most 0.0047.
Values may be sent and summed in bfloat16 or wider, within the bound.
No kernel may reach another device: no remote copies, remote signals or barrier semaphores. Data moves between devices by JAX's collectives and lax.ppermute only.
A program may use at most 64 MiB of HBM per device.

v0:
```python
import jax
import jax.numpy as jnp
from jax import lax
from jax.sharding import PartitionSpec as P

HALF = 12


epsilon = 1e-06


def passed_along(block, axis, distance):
    devices = range(lax.axis_size(axis))
    route = [(i - distance, i) for i in devices if i - distance in devices]
    return lax.ppermute(block, axis, route)


def band_matrix(filter_taps, samples):
    half_taps = (filter_taps.shape[0] - 1) // 2
    period = 2 * samples - 1
    spread = jnp.zeros((period,), jnp.float32)
    spread = lax.dynamic_update_slice(
        spread, filter_taps.astype(jnp.float32), (samples - 1 - half_taps,)
    )
    repeated = jnp.tile(spread, samples + 1)[: samples * (period + 1)]
    hankel = repeated.reshape(samples, period + 1)[:, :samples]
    return hankel[:, ::-1].astype(jnp.bfloat16)


def correlate_all(own_block, own_scale, stacked_partners, weights):
    count, events, samples = stacked_partners.shape
    partner_scale = lax.rsqrt(
        jnp.sum(jnp.square(stacked_partners.astype(jnp.float32)), axis=2) + epsilon
    )
    flat = stacked_partners.reshape(count * events, samples)
    own_padded = jnp.pad(own_block, ((0, 0), (HALF, HALF)))
    products = []
    for lag_index in range(2 * HALF + 1):
        start = 2 * HALF - lag_index
        shifted_own = own_padded[:, start : start + samples]
        product = lax.dot_general(
            shifted_own, flat, (((1,), (1,)), ((), ())), preferred_element_type=jnp.float32
        )
        products.append(product.reshape(events, count, events))
    stacked = jnp.stack(products, axis=2)
    scaled = (
        stacked
        * own_scale[:, None, None, None]
        * partner_scale[None, :, None, :]
        * weights[None, :, None, None]
    )
    return scaled.astype(jnp.bfloat16)


def shards(records, filter_taps, live_counts, pair_valid):
    events, samples = records.shape
    partner_count = pair_valid.shape[1]
    row_index = lax.broadcasted_iota(jnp.int32, (events, 1), 0)
    kept_rows = jnp.where(row_index < live_counts[0], records, jnp.zeros((), records.dtype))
    matrix = band_matrix(filter_taps, samples)
    own_block = jnp.dot(kept_rows, matrix, preferred_element_type=jnp.float32).astype(jnp.bfloat16)
    own_scale = lax.rsqrt(jnp.sum(jnp.square(own_block.astype(jnp.float32)), axis=1) + epsilon)
    partners = []
    for distance in range(1, partner_count + 1):
        partners.append(passed_along(own_block, "ev", -distance))
    stacked_partners = jnp.stack([own_block] + partners, axis=0)
    weights = jnp.concatenate(
        [jnp.ones((1,), jnp.float32), pair_valid[0].astype(jnp.float32)], axis=0
    )
    return correlate_all(own_block, own_scale, stacked_partners, weights)


def solution(mesh):
    in_specs = (P("ev", None), P(), P("ev"), P("ev", None))
    out_specs = P("ev", None, None, None)
    return jax.shard_map(shards, mesh=mesh, in_specs=in_specs, out_specs=out_specs, check_vma=False)
```

profile of v0, /device:TPU:31, one launch (start us, length us, event | category | flops | bytes accessed | tf_op | source)
XLA Modules:
  0.0 69.6 jit_solution(5310782027050341694)
XLA Ops:
  0.0 0.7 %pad_convert_fusion = bf16[1023]{0:T(1024)(128)(2,1)S(1)} fusion(bf16[65]{0:T(256)(128)(2,1)} %param.5), kind=kLoop, calls=%fused_computation.142 | loop fusion | bytes 2176 | tf_op jit(solution)/shard_map/dynamic_update_slice | solution.py:22
  0.9 1.6 %tile.10 = bf16[524799]{0:T(1024)(128)(2,1)S(1)} reshape(bf16[513,1023]{1,0:T(8,128)(2,1)S(1)} %tile.4) | data formatting | bytes 2099196 | tf_op jit(solution)/shard_map/tile | solution.py:25
  3.1 1.6 %rev.3 = bf16[512,512]{1,0:T(8,128)(2,1)S(1)} reverse(bf16[512,512]{1,0:T(8,128)(2,1)S(1)} %slice.106), dimensions={1} | reverse | bytes 1048576 | tf_op jit(solution)/shard_map/rev | solution.py:27
  5.8 2.6 %collective-permute-start = (bf16[128,512]{1,0:T(8,128)(2,1)S(1)}, bf16[128,512]{1,0:T(8,128)(2,1)S(1)}, u32[]{:S(2)}, u32[]{:S(2)}) collective-permute-start(bf16[128,512]{1,0:T(8,128)(2,1)S(1)} %get-tuple-element.6), channel_id=1, source_target_pairs={{1,0},{2,1},{3,2},{4,3},{5,4},{6,5},{7,6},{8,7},{9,8},{10,9},{11,1... | collective-permute-start | bytes 393224 | tf_op jit(solution)/shard_map/ppermute | solution.py:15
  8.3 2.5 %collective-permute-start.1 = (bf16[128,512]{1,0:T(8,128)(2,1)S(1)}, bf16[128,512]{1,0:T(8,128)(2,1)S(1)}, u32[]{:S(2)}, u32[]{:S(2)}) collective-permute-start(bf16[128,512]{1,0:T(8,128)(2,1)S(1)} %get-tuple-element.6), channel_id=1, source_target_pairs={{2,0},{3,1},{4,2},{5,3},{6,4},{7,5},{8,6},{9,7},{10,8},{11,9},{12,... | collective-permute-start | bytes 393224 | tf_op jit(solution)/shard_map/ppermute | solution.py:15
  10.8 2.3 %collective-permute-start.2 = (bf16[128,512]{1,0:T(8,128)(2,1)S(1)}, bf16[128,512]{1,0:T(8,128)(2,1)S(1)}, u32[]{:S(2)}, u32[]{:S(2)}) collective-permute-start(bf16[128,512]{1,0:T(8,128)(2,1)S(1)} %get-tuple-element.6), channel_id=1, source_target_pairs={{3,0},{4,1},{5,2},{6,3},{7,4},{8,5},{9,6},{10,7},{11,8},{12,9},{13... | collective-permute-start | bytes 393224 | tf_op jit(solution)/shard_map/ppermute | solution.py:15
  13.2 10.7 %collective-permute-start.3 = (bf16[128,512]{1,0:T(8,128)(2,1)S(1)}, bf16[128,512]{1,0:T(8,128)(2,1)S(1)}, u32[]{:S(2)}, u32[]{:S(2)}) collective-permute-start(bf16[128,512]{1,0:T(8,128)(2,1)S(1)} %get-tuple-element.6), channel_id=1, source_target_pairs={{4,0},{5,1},{6,2},{7,3},{8,4},{9,5},{10,6},{11,7},{12,8},{13,9},{1... | collective-permute-start | bytes 393224 | tf_op jit(solution)/shard_map/ppermute | solution.py:15
  23.9 2.5 %collective-permute-start.4 = (bf16[128,512]{1,0:T(8,128)(2,1)S(1)}, bf16[128,512]{1,0:T(8,128)(2,1)S(1)}, u32[]{:S(2)}, u32[]{:S(2)}) collective-permute-start(bf16[128,512]{1,0:T(8,128)(2,1)S(1)} %get-tuple-element.6), channel_id=1, source_target_pairs={{5,0},{6,1},{7,2},{8,3},{9,4},{10,5},{11,6},{12,7},{13,8},{14,9},{... | collective-permute-start | bytes 393224 | tf_op jit(solution)/shard_map/ppermute | solution.py:15
  26.6 4.2 %collective-permute-start.5 = (bf16[128,512]{1,0:T(8,128)(2,1)S(1)}, bf16[128,512]{1,0:T(8,128)(2,1)S(1)}, u32[]{:S(2)}, u32[]{:S(2)}) collective-permute-start(bf16[128,512]{1,0:T(8,128)(2,1)S(1)} %get-tuple-element.6), channel_id=1, source_target_pairs={{6,0},{7,1},{8,2},{9,3},{10,4},{11,5},{12,6},{13,7},{14,8},{15,9},... | collective-permute-start | bytes 393224 | tf_op jit(solution)/shard_map/ppermute | solution.py:15
  30.8 2.2 %collective-permute-start.6 = (bf16[128,512]{1,0:T(8,128)(2,1)S(1)}, bf16[128,512]{1,0:T(8,128)(2,1)S(1)}, u32[]{:S(2)}, u32[]{:S(2)}) collective-permute-start(bf16[128,512]{1,0:T(8,128)(2,1)S(1)} %get-tuple-element.6), channel_id=1, source_target_pairs={{7,0},{8,1},{9,2},{10,3},{11,4},{12,5},{13,6},{14,7},{15,8},{16,9}... | collective-permute-start | bytes 393224 | tf_op jit(solution)/shard_map/ppermute | solution.py:15
  33.1 2.6 %collective-permute-start.7 = (bf16[128,512]{1,0:T(8,128)(2,1)S(1)}, bf16[128,512]{1,0:T(8,128)(2,1)S(1)}, u32[]{:S(2)}, u32[]{:S(2)}) collective-permute-start(bf16[128,512]{1,0:T(8,128)(2,1)S(1)} %get-tuple-element.6), channel_id=1, source_target_pairs={{8,0},{9,1},{10,2},{11,3},{12,4},{13,5},{14,6},{15,7},{16,8},{17,9... | collective-permute-start | bytes 393224 | tf_op jit(solution)/shard_map/ppermute | solution.py:15
  35.8 2.9 %collective-permute-start.8 = (bf16[128,512]{1,0:T(8,128)(2,1)S(1)}, bf16[128,512]{1,0:T(8,128)(2,1)S(1)}, u32[]{:S(2)}, u32[]{:S(2)}) collective-permute-start(bf16[128,512]{1,0:T(8,128)(2,1)S(1)} %get-tuple-element.6), channel_id=1, source_target_pairs={{9,0},{10,1},{11,2},{12,3},{13,4},{14,5},{15,6},{16,7},{17,8},{18,... | collective-permute-start | bytes 393224 | tf_op jit(solution)/shard_map/ppermute | solution.py:15
  39.3 7.6 %collective-permute-done.8 = bf16[128,512]{1,0:T(8,128)(2,1)S(1)} collective-permute-done((bf16[128,512]{1,0:T(8,128)(2,1)S(1)}, bf16[128,512]{1,0:T(8,128)(2,1)S(1)}, u32[]{:S(2)}, u32[]{:S(2)}) %collective-permute-start.8) | collective-permute-done | bytes 131104 | tf_op jit(solution)/shard_map/ppermute | solution.py:15
  46.8 0.6 fusion.24
  47.7 0.6 fusion.23
  48.8 0.6 fusion.21
  50.0 0.6 fusion.19
  51.1 0.6 fusion.17
  51.7 0.6 fusion.16
  52.2 0.6 fusion.15
  52.8 0.6 fusion.14
  53.4 0.6 fusion.13
  54.5 0.6 fusion.11
  55.0 0.6 fusion.10
  55.6 0.6 fusion.9
  56.2 0.6 fusion.8
  56.7 0.6 fusion.7
  57.3 0.6 fusion.6
  57.9 0.6 fusion.5
  58.4 0.6 fusion.4
  61.3 3.2 %multiply_convert_fusion = bf16[128,10,25,128]{3,0,1,2:T(8,128)(2,1)S(1)} fusion(f32[128,10,25,128]{3,0,1,2:T(8,128)S(1)} %fusion, f32[10]{0:T(128)S(1)} %pad_maximum_fusion, f32[10,128]{1,0:T(8,128)S(1)} %add_rsqrt_fusion, f32[128]{0:T(128)S(1)} %add_rsqrt_fusion.1), kind=kLoop, calls=%fused_computation | loop fusion | flops 16384000 | bytes 24581672 | tf_op jit(solution)/shard_map/convert_element_type | solution.py:52
  64.4 5.2 %copy.5 = bf16[128,10,25,128]{3,0,2,1:T(8,128)(2,1)} copy(bf16[128,10,25,128]{3,0,1,2:T(8,128)(2,1)S(1)} %multiply_convert_fusion) | data formatting | bytes 16384000 | tf_op jit(solution)/shard_map/convert_element_type | solution.py:52
  (41 shorter events, 6.6 us)
Async XLA Ops:
  3.1 2.4 %copy-start = (bf16[128,512]{1,0:T(8,128)(2,1)S(1)}, bf16[128,512]{1,0:T(8,128)(2,1)}, u32[]{:S(2)}) copy-start(bf16[128,512]{1,0:T(8,128)(2,1)} %param.4) | copy-start | bytes 393220
  3.1 23.4 %copy-start.1 = (s32[1,9]{1,0:T(1,128)S(1)}, s32[1,9]{1,0:T(1,128)}, u32[]{:S(2)}) copy-start(s32[1,9]{1,0:T(1,128)} %param.7) | copy-start | bytes 112
  5.8 20.9 %collective-permute-start = (bf16[128,512]{1,0:T(8,128)(2,1)S(1)}, bf16[128,512]{1,0:T(8,128)(2,1)S(1)}, u32[]{:S(2)}, u32[]{:S(2)}) collective-permute-start(bf16[128,512]{1,0:T(8,128)(2,1)S(1)} %get-tuple-element.6), channel_id=1, source_target_pairs={{1,0},{2,1},{3,2},{4,3},{5,4},{6,5},{7,6},{8,7},{9,8},{10,9},{11,1... | collective-permute-start | bytes 393224 | tf_op jit(solution)/shard_map/ppermute | solution.py:15
  8.3 22.5 %collective-permute-start.1 = (bf16[128,512]{1,0:T(8,128)(2,1)S(1)}, bf16[128,512]{1,0:T(8,128)(2,1)S(1)}, u32[]{:S(2)}, u32[]{:S(2)}) collective-permute-start(bf16[128,512]{1,0:T(8,128)(2,1)S(1)} %get-tuple-element.6), channel_id=1, source_target_pairs={{2,0},{3,1},{4,2},{5,3},{6,4},{7,5},{8,6},{9,7},{10,8},{11,9},{12,... | collective-permute-start | bytes 393224 | tf_op jit(solution)/shard_map/ppermute | solution.py:15
  10.8 22.3 %collective-permute-start.2 = (bf16[128,512]{1,0:T(8,128)(2,1)S(1)}, bf16[128,512]{1,0:T(8,128)(2,1)S(1)}, u32[]{:S(2)}, u32[]{:S(2)}) collective-permute-start(bf16[128,512]{1,0:T(8,128)(2,1)S(1)} %get-tuple-element.6), channel_id=1, source_target_pairs={{3,0},{4,1},{5,2},{6,3},{7,4},{8,5},{9,6},{10,7},{11,8},{12,9},{13... | collective-permute-start | bytes 393224 | tf_op jit(solution)/shard_map/ppermute | solution.py:15
  13.2 22.6 %collective-permute-start.3 = (bf16[128,512]{1,0:T(8,128)(2,1)S(1)}, bf16[128,512]{1,0:T(8,128)(2,1)S(1)}, u32[]{:S(2)}, u32[]{:S(2)}) collective-permute-start(bf16[128,512]{1,0:T(8,128)(2,1)S(1)} %get-tuple-element.6), channel_id=1, source_target_pairs={{4,0},{5,1},{6,2},{7,3},{8,4},{9,5},{10,6},{11,7},{12,8},{13,9},{1... | collective-permute-start | bytes 393224 | tf_op jit(solution)/shard_map/ppermute | solution.py:15
  23.9 14.8 %collective-permute-start.4 = (bf16[128,512]{1,0:T(8,128)(2,1)S(1)}, bf16[128,512]{1,0:T(8,128)(2,1)S(1)}, u32[]{:S(2)}, u32[]{:S(2)}) collective-permute-start(bf16[128,512]{1,0:T(8,128)(2,1)S(1)} %get-tuple-element.6), channel_id=1, source_target_pairs={{5,0},{6,1},{7,2},{8,3},{9,4},{10,5},{11,6},{12,7},{13,8},{14,9},{... | collective-permute-start | bytes 393224 | tf_op jit(solution)/shard_map/ppermute | solution.py:15
  26.6 12.1 %collective-permute-start.5 = (bf16[128,512]{1,0:T(8,128)(2,1)S(1)}, bf16[128,512]{1,0:T(8,128)(2,1)S(1)}, u32[]{:S(2)}, u32[]{:S(2)}) collective-permute-start(bf16[128,512]{1,0:T(8,128)(2,1)S(1)} %get-tuple-element.6), channel_id=1, source_target_pairs={{6,0},{7,1},{8,2},{9,3},{10,4},{11,5},{12,6},{13,7},{14,8},{15,9},... | collective-permute-start | bytes 393224 | tf_op jit(solution)/shard_map/ppermute | solution.py:15
  30.8 7.9 %collective-permute-start.6 = (bf16[128,512]{1,0:T(8,128)(2,1)S(1)}, bf16[128,512]{1,0:T(8,128)(2,1)S(1)}, u32[]{:S(2)}, u32[]{:S(2)}) collective-permute-start(bf16[128,512]{1,0:T(8,128)(2,1)S(1)} %get-tuple-element.6), channel_id=1, source_target_pairs={{7,0},{8,1},{9,2},{10,3},{11,4},{12,5},{13,6},{14,7},{15,8},{16,9}... | collective-permute-start | bytes 393224 | tf_op jit(solution)/shard_map/ppermute | solution.py:15
  33.1 6.2 %collective-permute-start.7 = (bf16[128,512]{1,0:T(8,128)(2,1)S(1)}, bf16[128,512]{1,0:T(8,128)(2,1)S(1)}, u32[]{:S(2)}, u32[]{:S(2)}) collective-permute-start(bf16[128,512]{1,0:T(8,128)(2,1)S(1)} %get-tuple-element.6), channel_id=1, source_target_pairs={{8,0},{9,1},{10,2},{11,3},{12,4},{13,5},{14,6},{15,7},{16,8},{17,9... | collective-permute-start | bytes 393224 | tf_op jit(solution)/shard_map/ppermute | solution.py:15
  35.8 11.1 %collective-permute-start.8 = (bf16[128,512]{1,0:T(8,128)(2,1)S(1)}, bf16[128,512]{1,0:T(8,128)(2,1)S(1)}, u32[]{:S(2)}, u32[]{:S(2)}) collective-permute-start(bf16[128,512]{1,0:T(8,128)(2,1)S(1)} %get-tuple-element.6), channel_id=1, source_target_pairs={{9,0},{10,1},{11,2},{12,3},{13,4},{14,5},{15,6},{16,7},{17,8},{18,... | collective-permute-start | bytes 393224 | tf_op jit(solution)/shard_map/ppermute | solution.py:15
where the time goes:
time: 70 us; the launch traced here: 69.6 us
  starting transfers between devices  32.5 us (46%)
  matrix products  14.2 us (20%)
  local copies, waits for them, and re-layouts  10 us (14%)
  waiting for transfers between devices  8.06 us (12%)
  other arithmetic  3.71 us (5%)
  between operations  1.15 us (2%)
    ppermute x9, starting transfers between devices, passed_along(): return lax.ppermute(block, axis, route)  32.5 us
    dot_general x25, matrix products, correlate_all(): lax.dot_general(shifted_own, flat, (((1,), (1,)), ((), ())), preferred_el...  13.9 us
    ppermute x9, waiting for transfers between devices, passed_along(): return lax.ppermute(block, axis, route)  8.06 us
    convert_element_type x1, local copies, waits for them, and re-layouts, correlate_all(): return scaled.astype(jnp.bfloat16)  5.18 us
    convert_element_type x1, other arithmetic, correlate_all(): return scaled.astype(jnp.bfloat16)  3.18 us
    another operation x2, local copies, waits for them, and re-layouts, band_matrix(): repeated = jnp.tile(spread, samples + 1)[:samples * (period + 1)]  1.75 us
    rev x1, local copies, waits for them, and re-layouts, band_matrix(): return hankel[:, ::-1].astype(jnp.bfloat16)  1.65 us
  transfers between devices with their start and end apart: 9, of which 2 were waited for; matrix products, arithmetic and copies ran while one was open for 0% of the time, Pallas kernels for 0%

commit v1 on v0

v1 whole, which is shorter than its diff:
```python
import functools

import jax
import jax.numpy as jnp
from jax import lax
from jax.experimental import pallas as pl
from jax.experimental.pallas import tpu as pltpu
from jax.sharding import PartitionSpec as P


HALF = 12
LAGS = 2 * HALF + 1
EPSILON = 1e-06
LANES = 128
CHUNK = 5
VMEM_MIB = 16


VMEM = pl.BlockSpec(memory_space=pltpu.VMEM)
SMEM = pl.BlockSpec(memory_space=pltpu.SMEM)
ANY = pl.BlockSpec(memory_space=pl.ANY)
HBM = pl.BlockSpec(memory_space=pltpu.HBM)


def in_hbm(array):
    return pltpu.with_memory_space_constraint(array, pltpu.HBM)


def params():
    return pltpu.CompilerParams(vmem_limit_bytes=VMEM_MIB << 20)


def filter_kernel(live_ref, taps_hbm, records_hbm, own_ref, taps_ref, records_ref, row_ref, band_ref, sems):
    events, samples = records_ref.shape
    copies = [
        pltpu.make_async_copy(source, target, sems.at[i])
        for i, (source, target) in enumerate(
            ((taps_hbm, taps_ref), (records_hbm, records_ref))
        )
    ]
    for copy in copies:
        copy.start()
    copies[0].wait()
    taps = taps_ref.shape[1]
    half_taps = (taps - 1) // 2
    row_ref[...] = jnp.zeros_like(row_ref)
    row_ref[0:1, 0:taps] = taps_ref[...].astype(jnp.float32)
    first = pltpu.roll(row_ref[0:1, :], LANES - half_taps, 1)
    spread = jnp.broadcast_to(first, (LANES, LANES))
    circulant = pltpu.roll(spread, 0, 1, stride=1, stride_axis=0)
    t = lax.broadcasted_iota(jnp.int32, (LANES, LANES), 0)
    u = lax.broadcasted_iota(jnp.int32, (LANES, LANES), 1)
    zero = jnp.zeros((), jnp.float32)
    ahead = u - t
    near = jnp.where(jnp.abs(ahead) <= half_taps, circulant, zero).astype(jnp.bfloat16)
    before = jnp.where(ahead >= LANES - half_taps, circulant, zero).astype(jnp.bfloat16)
    after = jnp.where(ahead <= half_taps - LANES, circulant, zero).astype(jnp.bfloat16)
    none = jnp.zeros((LANES, LANES), jnp.bfloat16)
    tiles = samples // LANES
    for i in range(tiles):
        for j in range(tiles):
            tile = {0: near, -1: before, 1: after}.get(j - i, none)
            band_ref[i * LANES : (i + 1) * LANES, j * LANES : (j + 1) * LANES] = tile
    copies[1].wait()
    row = lax.broadcasted_iota(jnp.int32, (events, samples), 0)
    records = records_ref[...]
    kept = jnp.where(row < live_ref[0], records, jnp.zeros((), records.dtype))
    own_ref[...] = lax.dot_general(
        kept, band_ref[...], (((1,), (1,)), ((), ())), preferred_element_type=jnp.float32
    ).astype(jnp.bfloat16)


def filtered(records, filter_taps, live_counts):
    events, samples = records.shape
    return pl.pallas_call(
        filter_kernel,
        out_shape=jax.ShapeDtypeStruct((events, samples), jnp.bfloat16),
        in_specs=[SMEM, HBM, HBM],
        out_specs=VMEM,
        scratch_shapes=[
            pltpu.VMEM((1, filter_taps.shape[0]), jnp.bfloat16),
            pltpu.VMEM((events, samples), jnp.bfloat16),
            pltpu.VMEM((8, LANES), jnp.float32),
            pltpu.VMEM((samples, samples), jnp.bfloat16),
            pltpu.SemaphoreType.DMA((2,)),
        ],
        compiler_params=params(),
        name="filter_rows",
    )(live_counts, in_hbm(filter_taps.reshape(1, -1)), in_hbm(records))


def shift_kernel(count, valid_hbm, own_ref, shifted_ref, scale_ref, weight_ref, valid_ref, sem):
    events, samples = own_ref.shape
    copy = pltpu.make_async_copy(valid_hbm, valid_ref, sem)
    copy.start()
    own = own_ref[...].astype(jnp.float32)
    total = jnp.sum(own * own, axis=1, keepdims=True)
    scale_ref[...] = jnp.broadcast_to(lax.rsqrt(total + EPSILON), scale_ref.shape)
    padded = jnp.concatenate([own, jnp.zeros((events, LANES), jnp.float32)], axis=1)
    width = samples + LANES
    for lag in range(LAGS):
        moved = pltpu.roll(padded, (lag - HALF) % width, 1)[:, :samples]
        shifted_ref[lag * events : (lag + 1) * events, :] = moved.astype(jnp.bfloat16)
    copy.wait()
    me = lax.axis_index("ev")
    weight_ref[0:1, :] = jnp.ones((1, LANES), jnp.float32)
    for k in range(1, valid_hbm.shape[1] + 1):
        weight = jnp.where(me + k < count, valid_ref[0, k - 1].astype(jnp.float32), 0.0)
        weight_ref[k : k + 1, :] = jnp.full((1, LANES), weight, jnp.float32)


def shifted_rows(own, pair_valid, count):
    events, samples = own.shape
    slabs = pair_valid.shape[1] + 1
    return pl.pallas_call(
        functools.partial(shift_kernel, count),
        out_shape=(
            jax.ShapeDtypeStruct((LAGS * events, samples), jnp.bfloat16),
            jax.ShapeDtypeStruct((events, LANES), jnp.float32),
            jax.ShapeDtypeStruct((slabs, LANES), jnp.float32),
        ),
        in_specs=[HBM, VMEM],
        out_specs=(VMEM, VMEM, VMEM),
        scratch_shapes=[pltpu.SMEM(pair_valid.shape, jnp.int32), pltpu.SemaphoreType.DMA],
        compiler_params=params(),
        cost_estimate=pl.CostEstimate(flops=0, transcendentals=0, bytes_accessed=3 << 20),
        name="shift_rows",
    )(in_hbm(pair_valid), own)


def row_scale(block):
    square = jnp.square(block.astype(jnp.float32))
    high = square.astype(jnp.bfloat16)
    low = (square - high.astype(jnp.float32)).astype(jnp.bfloat16)
    ones = jnp.ones((8, block.shape[1]), jnp.bfloat16)
    over = (((1,), (1,)), ((), ()))
    total = lax.dot_general(ones, high, over, preferred_element_type=jnp.float32)
    total += lax.dot_general(ones, low, over, preferred_element_type=jnp.float32)
    return lax.rsqrt(total[0:1] + EPSILON)


def slots_of(slabs):
    core = lax.rem(lax.axis_index("ev"), 2)
    return [k if isinstance(k, int) else jnp.where(core == 0, k[0], k[1]) for k in slabs]


def pair_kernel(slabs, places, before, parts, last, shifted_ref, scale_ref, weight_ref, one_ref, two_ref, *rest):
    rest = list(rest)
    before_ref = None
    if before is not None:
        before_ref = rest.pop(0)
        rest.pop(0)
    out_ref, block_ref, factor_ref, before_sems, sems = rest
    events = scale_ref.shape[0]
    copies = []
    if before is not None:
        for i, k in enumerate(slots_of(before)):
            copy = pltpu.make_async_copy(before_ref.at[i], out_ref.at[k], before_sems.at[i])
            copy.start()
            copies.append(copy)
    always = lax.axis_index("ev") >= 0
    slots = slots_of(slabs)
    blocks = [ref if place is None else ref.at[place] for ref, place in zip((one_ref, two_ref), places)]

    def compute(start, stop, begin):
        partners = jnp.concatenate([block[...] for block in blocks], axis=0)
        if begin:
            scales = row_scale(partners)
            for i, k in enumerate(slots):
                part = scales[:, i * events : (i + 1) * events] * weight_ref[pl.ds(k, 1), :]
                factor_ref[i] = scale_ref[...] * part
        for low in range(start, stop, CHUNK):
            lags = slice(low, low + CHUNK)
            product = lax.dot_general(
                shifted_ref[low * events : (low + CHUNK) * events, :],
                partners,
                (((1,), (1,)), ((), ())),
                preferred_element_type=jnp.float32,
            )
            for i in range(2):
                piece = product[:, i * events : (i + 1) * events].reshape(CHUNK, events, events)
                block_ref[i, lags] = (piece * factor_ref[i][None]).astype(jnp.bfloat16)

    for n, (start, stop) in enumerate(parts):
        pl.when(always)(functools.partial(compute, start, stop, n == 0))
        if last:
            for i, k in enumerate(slots):
                copy = pltpu.make_async_copy(
                    block_ref.at[i, start:stop], out_ref.at[k, start:stop], sems.at[i, n]
                )
                copy.start()
                copies.append(copy)
    for copy in copies:
        copy.wait()


def correlate_pair(carried, slabs, blocks, places, held, last=False):
    shifted, scale, weight = held
    events = scale.shape[0]
    operands = [shifted, scale, weight, *blocks]
    in_specs = [VMEM] * 5
    aliases = {}
    before = None
    if carried is not None:
        out, before, block = carried
        operands += [block, out]
        in_specs += [VMEM, ANY]
        aliases = {6: 0}
    parts = ((0, 10), (10, 20), (20, LAGS)) if last else ((0, LAGS),)
    block = (2, LAGS, events, events)
    out_shape = [jax.ShapeDtypeStruct((weight.shape[0], LAGS, events, events), jnp.bfloat16)]
    out_specs = [ANY]
    scratch = [
        pltpu.VMEM((2, events, events), jnp.float32),
        pltpu.SemaphoreType.DMA((2,)),
        pltpu.SemaphoreType.DMA((2, len(parts))),
    ]
    if last:
        scratch.insert(0, pltpu.VMEM(block, jnp.bfloat16))
    else:
        out_shape.append(jax.ShapeDtypeStruct(block, jnp.bfloat16))
        out_specs.append(VMEM)
    result = pl.pallas_call(
        functools.partial(pair_kernel, slabs, places, before, parts, last),
        out_shape=out_shape,
        in_specs=in_specs,
        out_specs=out_specs,
        scratch_shapes=scratch,
        input_output_aliases=aliases,
        compiler_params=params(),
        cost_estimate=pl.CostEstimate(
            flops=4 * LAGS * events * events * shifted.shape[1],
            transcendentals=0,
            bytes_accessed=4 * LAGS * events * events,
        ),
        name="pair",
    )(*operands)
    return (result[0], slabs, None if last else result[1])


def permuted(block, target):
    count = lax.axis_size("ev")
    return lax.ppermute(block, "ev", [(s, target(s) % count) for s in range(count)])


def along_row(step):
    def target(s):
        return s // 8 * 8 + (s % 8 - 2 * step) % 8

    return target


def whole(records, filter_taps, live_counts, pair_valid):
    count = lax.axis_size("ev")
    own = filtered(records, filter_taps, live_counts)
    chip = lax.rem(lax.axis_index("ev") // 2, 4)

    above = permuted(own, lambda s: s - 8)
    mixed = permuted(own, lambda s: s - 1 if s % 2 else s - 9)
    held = shifted_rows(own, pair_valid, count)

    def swapped(block):
        return permuted(block, lambda s: s ^ 1)

    def ahead(step):
        payload = jnp.where(chip >= step, own, above)
        return permuted(payload, along_row(step))

    x1 = ahead(1)
    x3 = ahead(3)
    x2 = ahead(2)
    three_s = swapped(jnp.stack([above, x1, x3]))
    x2_s = swapped(x2)
    none = (None, None)
    carried = correlate_pair(None, (0, 8), (own, above), none, held)
    carried = correlate_pair(carried, (2, 6), (x1, x3), none, held)
    carried = correlate_pair(carried, ((1, 9), (9, 7)), (mixed, three_s), (None, 0), held)
    carried = correlate_pair(carried, ((3, 1), (7, 5)), (three_s, three_s), (1, 2), held)
    carried = correlate_pair(carried, (4, (5, 3)), (x2, x2_s), none, held, last=True)
    return carried[0].transpose(2, 0, 1, 3)


def solution(mesh):
    in_specs = (P("ev", None), P(), P("ev"), P("ev", None))
    out_specs = P("ev", None, None, None)
    return jax.shard_map(whole, mesh=mesh, in_specs=in_specs, out_specs=out_specs, check_vma=False)
```

time: 70 us -> 38.1 us (0.54)
  the two profiles are of different devices: /device:TPU:31 before, /device:TPU:7 now
where the time goes in v1:
time: 38.1 us; the launch traced here: 38 us
  starting transfers between devices  20.3 us (53%)
  Pallas kernels  9.72 us (26%)
  waiting for transfers between devices  7.15 us (19%)
  between operations  0.74 us (2%)
    ppermute x7, starting transfers between devices, permuted(): lax.ppermute(block, 'ev', [(s, target(s) % count) for s in range(count)])  20.3 us
    pallas_call x5, Pallas kernels, correlate_pair(): pl.pallas_call(functools.partial(pair_kernel, slabs, places, before, part...  7.46 us
    ppermute x7, waiting for transfers between devices, permuted(): lax.ppermute(block, 'ev', [(s, target(s) % count) for s in range(count)])  7.15 us
    pallas_call x1, Pallas kernels, filtered(): pl.pallas_call(filter_kernel, out_shape=jax.ShapeDtypeStruct((events, sam...  1.25 us
    pallas_call x1, Pallas kernels, shifted_rows(): pl.pallas_call(functools.partial(shift_kernel, count), out_shape=(jax.Sha...  1.02 us
  transfers between devices with their start and end apart: 7, of which 3 were waited for; matrix products, arithmetic and copies ran while one was open for 0% of the time, Pallas kernels for 16%

profile of v1, /device:TPU:7, one launch (start us, length us, event | category | flops | bytes accessed | tf_op | source)
XLA Modules:
  0.0 38.0 jit_solution(15395208955955919354)
XLA Ops:
  0.7 1.2 %filter_rows.1.own_ref.one_ref = bf16[128,512]{1,0:T(8,128)(2,1)S(1)} custom-call(s32[1]{0:T(128)S(6)} %copy.13.live_ref, bf16[1,65]{1,0:T(2,128)(2,1)} %bitcast.8, bf16[128,512]{1,0:T(8,128)(2,1)} %records_hbm.1), custom_call_target="tpu_custom_call" | custom-call | tf_op jit(solution)/shard_map/filter_rows/pallas_call | solution.py:75
  1.9 8.1 %collective-permute-start = (bf16[128,512]{1,0:T(8,128)(2,1)S(1)}, bf16[128,512]{1,0:T(8,128)(2,1)S(1)}, u32[]{:S(2)}, u32[]{:S(2)}) collective-permute-start(bf16[128,512]{1,0:T(8,128)(2,1)S(1)} %filter_rows.1.own_ref.one_ref), channel_id=1, source_target_pairs={{0,248},{1,249},{2,250},{3,251},{4,252},{5,253},{6,254},{7,255},{8... | collective-permute-start | bytes 393224 | tf_op jit(solution)/shard_map/ppermute | solution.py:243
  10.0 2.2 %collective-permute-done.two_ref = bf16[128,512]{1,0:T(8,128)(2,1)S(1)} collective-permute-done((bf16[128,512]{1,0:T(8,128)(2,1)S(1)}, bf16[128,512]{1,0:T(8,128)(2,1)S(1)}, u32[]{:S(2)}, u32[]{:S(2)}) %collective-permute-start) | collective-permute-done | bytes 131104 | tf_op jit(solution)/shard_map/ppermute | solution.py:243
  12.2 0.6 %collective-permute-start.3 = (bf16[128,512]{1,0:T(8,128)(2,1)S(1)}, bf16[128,512]{1,0:T(8,128)(2,1)S(1)}, u32[]{:S(2)}, u32[]{:S(2)}) collective-permute-start(bf16[128,512]{1,0:T(8,128)(2,1)S(1)} %get-tuple-element.27), channel_id=1, source_target_pairs={{0,6},{1,7},{2,0},{3,1},{4,2},{5,3},{6,4},{7,5},{8,14},{9,15},{10,... | collective-permute-start | bytes 393224 | tf_op jit(solution)/shard_map/ppermute | solution.py:243
  12.8 2.1 %collective-permute-start.4 = (bf16[128,512]{1,0:T(8,128)(2,1)S(1)}, bf16[128,512]{1,0:T(8,128)(2,1)S(1)}, u32[]{:S(2)}, u32[]{:S(2)}) collective-permute-start(bf16[128,512]{1,0:T(8,128)(2,1)S(1)} %get-tuple-element.28), channel_id=1, source_target_pairs={{0,2},{1,3},{2,4},{3,5},{4,6},{5,7},{6,0},{7,1},{8,10},{9,11},{10,... | collective-permute-start | bytes 393224 | tf_op jit(solution)/shard_map/ppermute | solution.py:243
  15.0 2.4 %collective-permute-done.3.one_ref = bf16[128,512]{1,0:T(8,128)(2,1)S(1)} collective-permute-done((bf16[128,512]{1,0:T(8,128)(2,1)S(1)}, bf16[128,512]{1,0:T(8,128)(2,1)S(1)}, u32[]{:S(2)}, u32[]{:S(2)}) %collective-permute-start.3) | collective-permute-done | bytes 131104 | tf_op jit(solution)/shard_map/ppermute | solution.py:243
  17.3 0.0 collective-permute-done.4.two_ref
  17.4 2.8 %collective-permute-start.5 = (bf16[3,128,512]{2,1,0:T(8,128)(2,1)S(1)}, bf16[3,128,512]{2,1,0:T(8,128)(2,1)S(1)}, u32[]{:S(2)}, u32[]{:S(2)}) collective-permute-start(bf16[3,128,512]{2,1,0:T(8,128)(2,1)S(1)} %pad_maximum_fusion), channel_id=1, source_target_pairs={{0,1},{1,0},{2,3},{3,2},{4,5},{5,4},{6,7},{7,6},{8,9},{9,8},{10,11... | collective-permute-start | bytes 1179656 | tf_op jit(solution)/shard_map/ppermute | solution.py:243
  20.2 1.2 %collective-permute-start.1 = (bf16[128,512]{1,0:T(8,128)(2,1)S(1)}, bf16[128,512]{1,0:T(8,128)(2,1)S(1)}, u32[]{:S(2)}, u32[]{:S(2)}) collective-permute-start(bf16[128,512]{1,0:T(8,128)(2,1)S(1)} %get-tuple-element.29), channel_id=1, source_target_pairs={{0,4},{1,5},{2,6},{3,7},{4,0},{5,1},{6,2},{7,3},{8,12},{9,13},{10,... | collective-permute-start | bytes 393224 | tf_op jit(solution)/shard_map/ppermute | solution.py:243
  21.3 0.4 %collective-permute-start.6 = (bf16[128,512]{1,0:T(8,128)(2,1)S(1)}, bf16[128,512]{1,0:T(8,128)(2,1)S(1)}, u32[]{:S(2)}, u32[]{:S(2)}) collective-permute-start(bf16[128,512]{1,0:T(8,128)(2,1)S(1)} %filter_rows.1.own_ref.one_ref), channel_id=1, source_target_pairs={{0,247},{1,0},{2,249},{3,2},{4,251},{5,4},{6,253},{7,6},{8,255},{9... | collective-permute-start | bytes 393224 | tf_op jit(solution)/shard_map/ppermute | solution.py:243
  21.7 1.0 %shift_rows.1 = (bf16[3200,512]{1,0:T(8,128)(2,1)S(1)}, f32[128,128]{1,0:T(8,128)S(1)}, f32[10,128]{1,0:T(8,128)S(1)}) custom-call(s32[1,9]{1,0:T(1,128)} %valid_hbm.1, bf16[128,512]{1,0:T(8,128)(2,1)S(1)} %filter_rows.1.own_ref.one_ref), custom_call_target="tpu_custom_call" | custom-call | bytes 3145728 | tf_op jit(solution)/shard_map/shift_rows/pallas_call | solution.py:115
  22.7 1.3 %pair.5 = (bf16[10,25,128,128]{3,2,1,0:T(8,128)(2,1)}, bf16[2,25,128,128]{3,2,1,0:T(8,128)(2,1)S(1)}) custom-call(bf16[3200,512]{1,0:T(8,128)(2,1)S(1)} %get-tuple-element.16.shifted_ref, f32[128,128]{1,0:T(8,128)S(1)} %get-tuple-element.17.scale_ref, f32[10,128]{1,0:T(8,128)S(1)} %get-tuple-element.18.weight_ref, ...), custom_call_target="tpu_custom_call" | custom-call | flops 838860800 | bytes 1638400 | tf_op jit(solution)/shard_map/pair/pallas_call | solution.py:223
  24.0 2.6 %collective-permute-done.1.one_ref = bf16[128,512]{1,0:T(8,128)(2,1)S(1)} collective-permute-done((bf16[128,512]{1,0:T(8,128)(2,1)S(1)}, bf16[128,512]{1,0:T(8,128)(2,1)S(1)}, u32[]{:S(2)}, u32[]{:S(2)}) %collective-permute-start.1) | collective-permute-done | bytes 131104 | tf_op jit(solution)/shard_map/ppermute | solution.py:243
  26.6 5.1 %collective-permute-start.2 = (bf16[128,512]{1,0:T(8,128)(2,1)S(1)}, bf16[128,512]{1,0:T(8,128)(2,1)S(1)}, u32[]{:S(2)}, u32[]{:S(2)}) collective-permute-start(bf16[128,512]{1,0:T(8,128)(2,1)S(1)} %collective-permute-done.1.one_ref), channel_id=1, source_target_pairs={{0,1},{1,0},{2,3},{3,2},{4,5},{5,4},{6,7},{7,6},{8,9},{9,8},{10,11... | collective-permute-start | bytes 393224 | tf_op jit(solution)/shard_map/ppermute | solution.py:243
  31.7 1.2 %pair.6 = (bf16[10,25,128,128]{3,2,1,0:T(8,128)(2,1)}, bf16[2,25,128,128]{3,2,1,0:T(8,128)(2,1)S(1)}) custom-call(bf16[3200,512]{1,0:T(8,128)(2,1)S(1)} %get-tuple-element.16.shifted_ref, f32[128,128]{1,0:T(8,128)S(1)} %get-tuple-element.17.scale_ref, f32[10,128]{1,0:T(8,128)S(1)} %get-tuple-element.18.weight_ref, ...), custom_call_target="tpu_custom_call", output_to_operand_aliasing={{0}: (6, {})} | custom-call | flops 838860800 | bytes 1638400 | tf_op jit(solution)/shard_map/pair/pallas_call | solution.py:223
  33.0 0.0 collective-permute-done.6.one_ref
  33.0 0.0 collective-permute-done.5.two_ref.one_ref
  33.0 1.3 %pair.7 = (bf16[10,25,128,128]{3,2,1,0:T(8,128)(2,1)}, bf16[2,25,128,128]{3,2,1,0:T(8,128)(2,1)S(1)}) custom-call(bf16[3200,512]{1,0:T(8,128)(2,1)S(1)} %get-tuple-element.16.shifted_ref, f32[128,128]{1,0:T(8,128)S(1)} %get-tuple-element.17.scale_ref, f32[10,128]{1,0:T(8,128)S(1)} %get-tuple-element.18.weight_ref, ...), custom_call_target="tpu_custom_call", output_to_operand_aliasing={{0}: (6, {})} | custom-call | flops 838860800 | bytes 1638400 | tf_op jit(solution)/shard_map/pair/pallas_call | solution.py:223
  34.3 1.3 %pair.8 = (bf16[10,25,128,128]{3,2,1,0:T(8,128)(2,1)}, bf16[2,25,128,128]{3,2,1,0:T(8,128)(2,1)S(1)}) custom-call(bf16[3200,512]{1,0:T(8,128)(2,1)S(1)} %get-tuple-element.16.shifted_ref, f32[128,128]{1,0:T(8,128)S(1)} %get-tuple-element.17.scale_ref, f32[10,128]{1,0:T(8,128)S(1)} %get-tuple-element.18.weight_ref, ...), custom_call_target="tpu_custom_call", output_to_operand_aliasing={{0}: (6, {})} | custom-call | flops 838860800 | bytes 1638400 | tf_op jit(solution)/shard_map/pair/pallas_call | solution.py:223
  35.5 0.0 collective-permute-done.2.two_ref
  35.5 2.4 %pair.9 = bf16[10,25,128,128]{3,2,1,0:T(8,128)(2,1)} custom-call(bf16[3200,512]{1,0:T(8,128)(2,1)S(1)} %get-tuple-element.16.shifted_ref, f32[128,128]{1,0:T(8,128)S(1)} %get-tuple-element.17.scale_ref, f32[10,128]{1,0:T(8,128)S(1)} %get-tuple-element.18.weight_ref, ...), custom_call_target="tpu_custom_call", output_to_operand_aliasing={{}: (6, {})} | custom-call | flops 838860800 | bytes 1638400 | tf_op jit(solution)/shard_map/pair/pallas_call | solution.py:223
  (2 shorter events, 0.1 us)
Async XLA Ops:
  1.9 10.3 %collective-permute-start = (bf16[128,512]{1,0:T(8,128)(2,1)S(1)}, bf16[128,512]{1,0:T(8,128)(2,1)S(1)}, u32[]{:S(2)}, u32[]{:S(2)}) collective-permute-start(bf16[128,512]{1,0:T(8,128)(2,1)S(1)} %filter_rows.1.own_ref.one_ref), channel_id=1, source_target_pairs={{0,248},{1,249},{2,250},{3,251},{4,252},{5,253},{6,254},{7,255},{8... | collective-permute-start | bytes 393224 | tf_op jit(solution)/shard_map/ppermute | solution.py:243
  12.2 5.1 %collective-permute-start.3 = (bf16[128,512]{1,0:T(8,128)(2,1)S(1)}, bf16[128,512]{1,0:T(8,128)(2,1)S(1)}, u32[]{:S(2)}, u32[]{:S(2)}) collective-permute-start(bf16[128,512]{1,0:T(8,128)(2,1)S(1)} %get-tuple-element.27), channel_id=1, source_target_pairs={{0,6},{1,7},{2,0},{3,1},{4,2},{5,3},{6,4},{7,5},{8,14},{9,15},{10,... | collective-permute-start | bytes 393224 | tf_op jit(solution)/shard_map/ppermute | solution.py:243
  12.8 4.5 %collective-permute-start.4 = (bf16[128,512]{1,0:T(8,128)(2,1)S(1)}, bf16[128,512]{1,0:T(8,128)(2,1)S(1)}, u32[]{:S(2)}, u32[]{:S(2)}) collective-permute-start(bf16[128,512]{1,0:T(8,128)(2,1)S(1)} %get-tuple-element.28), channel_id=1, source_target_pairs={{0,2},{1,3},{2,4},{3,5},{4,6},{5,7},{6,0},{7,1},{8,10},{9,11},{10,... | collective-permute-start | bytes 393224 | tf_op jit(solution)/shard_map/ppermute | solution.py:243
  17.4 15.6 %collective-permute-start.5 = (bf16[3,128,512]{2,1,0:T(8,128)(2,1)S(1)}, bf16[3,128,512]{2,1,0:T(8,128)(2,1)S(1)}, u32[]{:S(2)}, u32[]{:S(2)}) collective-permute-start(bf16[3,128,512]{2,1,0:T(8,128)(2,1)S(1)} %pad_maximum_fusion), channel_id=1, source_target_pairs={{0,1},{1,0},{2,3},{3,2},{4,5},{5,4},{6,7},{7,6},{8,9},{9,8},{10,11... | collective-permute-start | bytes 1179656 | tf_op jit(solution)/shard_map/ppermute | solution.py:243
  20.2 6.5 %collective-permute-start.1 = (bf16[128,512]{1,0:T(8,128)(2,1)S(1)}, bf16[128,512]{1,0:T(8,128)(2,1)S(1)}, u32[]{:S(2)}, u32[]{:S(2)}) collective-permute-start(bf16[128,512]{1,0:T(8,128)(2,1)S(1)} %get-tuple-element.29), channel_id=1, source_target_pairs={{0,4},{1,5},{2,6},{3,7},{4,0},{5,1},{6,2},{7,3},{8,12},{9,13},{10,... | collective-permute-start | bytes 393224 | tf_op jit(solution)/shard_map/ppermute | solution.py:243
  21.3 11.6 %collective-permute-start.6 = (bf16[128,512]{1,0:T(8,128)(2,1)S(1)}, bf16[128,512]{1,0:T(8,128)(2,1)S(1)}, u32[]{:S(2)}, u32[]{:S(2)}) collective-permute-start(bf16[128,512]{1,0:T(8,128)(2,1)S(1)} %filter_rows.1.own_ref.one_ref), channel_id=1, source_target_pairs={{0,247},{1,0},{2,249},{3,2},{4,251},{5,4},{6,253},{7,6},{8,255},{9... | collective-permute-start | bytes 393224 | tf_op jit(solution)/shard_map/ppermute | solution.py:243
  26.6 8.9 %collective-permute-start.2 = (bf16[128,512]{1,0:T(8,128)(2,1)S(1)}, bf16[128,512]{1,0:T(8,128)(2,1)S(1)}, u32[]{:S(2)}, u32[]{:S(2)}) collective-permute-start(bf16[128,512]{1,0:T(8,128)(2,1)S(1)} %collective-permute-done.1.one_ref), channel_id=1, source_target_pairs={{0,1},{1,0},{2,3},{3,2},{4,5},{5,4},{6,7},{7,6},{8,9},{9,8},{10,11... | collective-permute-start | bytes 393224 | tf_op jit(solution)/shard_map/ppermute | solution.py:243

commit v2 on v1

--- a/solution.py
+++ b/solution.py
@@ -140,11 +140,19 @@
 
 
 def slots_of(slabs):
-    core = lax.rem(lax.axis_index("ev"), 2)
-    return [k if isinstance(k, int) else jnp.where(core == 0, k[0], k[1]) for k in slabs]
-
-
-def pair_kernel(slabs, places, before, parts, last, shifted_ref, scale_ref, weight_ref, one_ref, two_ref, *rest):
+    place = lax.rem(lax.axis_index("ev"), 4)
+
+    def slot(k):
+        if isinstance(k, int):
+            return k
+        if len(k) == 2:
+            return jnp.where(lax.rem(place, 2) == 0, k[0], k[1])
+        return jnp.where(place == 0, k[0], jnp.where(place == 1, k[1], jnp.where(place == 2, k[2], k[3])))
+
+    return [slot(k) for k in slabs]
+
+
+def pair_kernel(slabs, places, before, parts, sent, shifted_ref, scale_ref, weight_ref, one_ref, two_ref, *rest):
     rest = list(rest)
     before_ref = None
     if before is not None:
@@ -154,8 +162,9 @@
     events = scale_ref.shape[0]
     copies = []
     if before is not None:
-        for i, k in enumerate(slots_of(before)):
-            copy = pltpu.make_async_copy(before_ref.at[i], out_ref.at[k], before_sems.at[i])
+        left = slice(before[1], LAGS)
+        for i, k in enumerate(slots_of(before[0])):
+            copy = pltpu.make_async_copy(before_ref.at[i, left], out_ref.at[k, left], before_sems.at[i])
             copy.start()
             copies.append(copy)
     always = lax.axis_index("ev") >= 0
@@ -183,7 +192,7 @@
 
     for n, (start, stop) in enumerate(parts):
         pl.when(always)(functools.partial(compute, start, stop, n == 0))
-        if last:
+        if n < sent:
             for i, k in enumerate(slots):
                 copy = pltpu.make_async_copy(
                     block_ref.at[i, start:stop], out_ref.at[k, start:stop], sems.at[i, n]
@@ -194,7 +203,7 @@
         copy.wait()
 
 
-def correlate_pair(carried, slabs, blocks, places, held, last=False):
+def correlate_pair(carried, slabs, blocks, places, held, parts=((0, LAGS),), sent=0):
     shifted, scale, weight = held
     events = scale.shape[0]
     operands = [shifted, scale, weight, *blocks]
@@ -206,7 +215,7 @@
         operands += [block, out]
         in_specs += [VMEM, ANY]
         aliases = {6: 0}
-    parts = ((0, 10), (10, 20), (20, LAGS)) if last else ((0, LAGS),)
+    last = sent == len(parts)
     block = (2, LAGS, events, events)
     out_shape = [jax.ShapeDtypeStruct((weight.shape[0], LAGS, events, events), jnp.bfloat16)]
     out_specs = [ANY]
@@ -221,7 +230,7 @@
         out_shape.append(jax.ShapeDtypeStruct(block, jnp.bfloat16))
         out_specs.append(VMEM)
     result = pl.pallas_call(
-        functools.partial(pair_kernel, slabs, places, before, parts, last),
+        functools.partial(pair_kernel, slabs, places, before, parts, sent),
         out_shape=out_shape,
         in_specs=in_specs,
         out_specs=out_specs,
@@ -235,7 +244,7 @@
         ),
         name="pair",
     )(*operands)
-    return (result[0], slabs, None if last else result[1])
+    return (result[0], (slabs, parts[sent - 1][1] if sent else 0), None if last else result[1])
 
 
 def permuted(block, target):
@@ -244,10 +253,7 @@
 
 
 def along_row(step):
-    def target(s):
-        return s // 8 * 8 + (s % 8 - 2 * step) % 8
-
-    return target
+    return lambda s: s ^ (2 * step)
 
 
 def whole(records, filter_taps, live_counts, pair_valid):
@@ -263,20 +269,22 @@
         return permuted(block, lambda s: s ^ 1)
 
     def ahead(step):
-        payload = jnp.where(chip >= step, own, above)
+        payload = jnp.where(chip > jnp.bitwise_xor(chip, step), own, above)
         return permuted(payload, along_row(step))
 
     x1 = ahead(1)
     x3 = ahead(3)
     x2 = ahead(2)
-    three_s = swapped(jnp.stack([above, x1, x3]))
-    x2_s = swapped(x2)
+    above_s = swapped(above)
+    x1_s = swapped(x1)
+    two_s = swapped(jnp.stack([x3, x2]))
     none = (None, None)
     carried = correlate_pair(None, (0, 8), (own, above), none, held)
-    carried = correlate_pair(carried, (2, 6), (x1, x3), none, held)
-    carried = correlate_pair(carried, ((1, 9), (9, 7)), (mixed, three_s), (None, 0), held)
-    carried = correlate_pair(carried, ((3, 1), (7, 5)), (three_s, three_s), (1, 2), held)
-    carried = correlate_pair(carried, (4, (5, 3)), (x2, x2_s), none, held, last=True)
+    carried = correlate_pair(carried, ((1, 9), (9, 7)), (mixed, above_s), none, held)
+    carried = correlate_pair(carried, ((2, 2, 6, 6), (3, 1, 7, 5)), (x1, x1_s), none, held)
+    carried = correlate_pair(carried, ((6, 6, 2, 2), 4), (x3, x2), none, held)
+    parts = ((0, 15), (15, LAGS))
+    carried = correlate_pair(carried, ((7, 5, 3, 1), (5, 3)), (two_s, two_s), (0, 1), held, parts, 2)
     return carried[0].transpose(2, 0, 1, 3)
 
 

time: 38.1 us -> 32.6 us (0.86)
  the two profiles are of different devices: /device:TPU:7 before, /device:TPU:1 now
where the time goes in v2:
time: 32.6 us; the launch traced here: 32.5 us
  starting transfers between devices  19.9 us (61%)
  Pallas kernels  9.64 us (30%)
  waiting for transfers between devices  2.2 us (7%)
  between operations  0.75 us (2%)
    ppermute x8, starting transfers between devices, permuted(): lax.ppermute(block, 'ev', [(s, target(s) % count) for s in range(count)])  19.9 us
    pallas_call x5, Pallas kernels, correlate_pair(): pl.pallas_call(functools.partial(pair_kernel, slabs, places, before, part...  7.37 us
    ppermute x8, waiting for transfers between devices, permuted(): lax.ppermute(block, 'ev', [(s, target(s) % count) for s in range(count)])  2.2 us
    pallas_call x1, Pallas kernels, filtered(): pl.pallas_call(filter_kernel, out_shape=jax.ShapeDtypeStruct((events, sam...  1.25 us
    pallas_call x1, Pallas kernels, shifted_rows(): pl.pallas_call(functools.partial(shift_kernel, count), out_shape=(jax.Sha...  1.02 us
  transfers between devices with their start and end apart: 8, of which 1 were waited for; matrix products, arithmetic and copies ran while one was open for 0% of the time, Pallas kernels for 19%

profile of v2, /device:TPU:1, one launch (start us, length us, event | category | flops | bytes accessed | tf_op | source)
XLA Modules:
  0.0 32.5 jit_solution(7551154352068252960)
XLA Ops:
  0.7 1.2 %filter_rows.1.own_ref.one_ref = bf16[128,512]{1,0:T(8,128)(2,1)S(1)} custom-call(s32[1]{0:T(128)S(6)} %copy.13.live_ref, bf16[1,65]{1,0:T(2,128)(2,1)} %bitcast.6, bf16[128,512]{1,0:T(8,128)(2,1)} %records_hbm.1), custom_call_target="tpu_custom_call" | custom-call | tf_op jit(solution)/shard_map/filter_rows/pallas_call | solution.py:75
  1.9 8.9 %collective-permute-start = (bf16[128,512]{1,0:T(8,128)(2,1)S(1)}, bf16[128,512]{1,0:T(8,128)(2,1)S(1)}, u32[]{:S(2)}, u32[]{:S(2)}) collective-permute-start(bf16[128,512]{1,0:T(8,128)(2,1)S(1)} %filter_rows.1.own_ref.one_ref), channel_id=1, source_target_pairs={{0,248},{1,249},{2,250},{3,251},{4,252},{5,253},{6,254},{7,255},{8... | collective-permute-start | bytes 393224 | tf_op jit(solution)/shard_map/ppermute | solution.py:252
  10.8 2.2 %collective-permute-done.two_ref = bf16[128,512]{1,0:T(8,128)(2,1)S(1)} collective-permute-done((bf16[128,512]{1,0:T(8,128)(2,1)S(1)}, bf16[128,512]{1,0:T(8,128)(2,1)S(1)}, u32[]{:S(2)}, u32[]{:S(2)}) %collective-permute-start) | collective-permute-done | bytes 131104 | tf_op jit(solution)/shard_map/ppermute | solution.py:252
  13.0 2.6 %collective-permute-start.1 = (bf16[128,512]{1,0:T(8,128)(2,1)S(1)}, bf16[128,512]{1,0:T(8,128)(2,1)S(1)}, u32[]{:S(2)}, u32[]{:S(2)}) collective-permute-start(bf16[128,512]{1,0:T(8,128)(2,1)S(1)} %get-tuple-element.29), channel_id=1, source_target_pairs={{0,6},{1,7},{2,4},{3,5},{4,2},{5,3},{6,0},{7,1},{8,14},{9,15},{10,... | collective-permute-start | bytes 393224 | tf_op jit(solution)/shard_map/ppermute | solution.py:252
  15.6 0.5 %collective-permute-start.2 = (bf16[128,512]{1,0:T(8,128)(2,1)S(1)}, bf16[128,512]{1,0:T(8,128)(2,1)S(1)}, u32[]{:S(2)}, u32[]{:S(2)}) collective-permute-start(bf16[128,512]{1,0:T(8,128)(2,1)S(1)} %get-tuple-element.28), channel_id=1, source_target_pairs={{0,4},{1,5},{2,6},{3,7},{4,0},{5,1},{6,2},{7,3},{8,12},{9,13},{10,... | collective-permute-start | bytes 393224 | tf_op jit(solution)/shard_map/ppermute | solution.py:252
  16.1 0.3 collective-permute-start.4
  16.4 2.4 %collective-permute-start.6 = (bf16[128,512]{1,0:T(8,128)(2,1)S(1)}, bf16[128,512]{1,0:T(8,128)(2,1)S(1)}, u32[]{:S(2)}, u32[]{:S(2)}) collective-permute-start(bf16[128,512]{1,0:T(8,128)(2,1)S(1)} %filter_rows.1.own_ref.one_ref), channel_id=1, source_target_pairs={{0,247},{1,0},{2,249},{3,2},{4,251},{5,4},{6,253},{7,6},{8,255},{9... | collective-permute-start | bytes 393224 | tf_op jit(solution)/shard_map/ppermute | solution.py:252
  18.8 1.0 %shift_rows.1 = (bf16[3200,512]{1,0:T(8,128)(2,1)S(1)}, f32[128,128]{1,0:T(8,128)S(1)}, f32[10,128]{1,0:T(8,128)S(1)}) custom-call(s32[1,9]{1,0:T(1,128)} %valid_hbm.1, bf16[128,512]{1,0:T(8,128)(2,1)S(1)} %filter_rows.1.own_ref.one_ref), custom_call_target="tpu_custom_call" | custom-call | bytes 3145728 | tf_op jit(solution)/shard_map/shift_rows/pallas_call | solution.py:115
  19.8 2.9 %collective-permute-start.7 = (bf16[128,512]{1,0:T(8,128)(2,1)S(1)}, bf16[128,512]{1,0:T(8,128)(2,1)S(1)}, u32[]{:S(2)}, u32[]{:S(2)}) collective-permute-start(bf16[128,512]{1,0:T(8,128)(2,1)S(1)} %collective-permute-done.two_ref), channel_id=1, source_target_pairs={{0,1},{1,0},{2,3},{3,2},{4,5},{5,4},{6,7},{7,6},{8,9},{9,8},{10,11... | collective-permute-start | bytes 393224 | tf_op jit(solution)/shard_map/ppermute | solution.py:252
  22.7 0.0 collective-permute-done.1.one_ref
  22.7 0.0 collective-permute-done.2.two_ref
  22.8 1.8 %collective-permute-start.3 = (bf16[2,128,512]{2,1,0:T(8,128)(2,1)S(1)}, bf16[2,128,512]{2,1,0:T(8,128)(2,1)S(1)}, u32[]{:S(2)}, u32[]{:S(2)}) collective-permute-start(bf16[2,128,512]{2,1,0:T(8,128)(2,1)S(1)} %pad_maximum_fusion), channel_id=1, source_target_pairs={{0,1},{1,0},{2,3},{3,2},{4,5},{5,4},{6,7},{7,6},{8,9},{9,8},{10,11... | collective-permute-start | bytes 786440 | tf_op jit(solution)/shard_map/ppermute | solution.py:252
  24.6 0.0 collective-permute-done.4.one_ref
  24.6 0.5 %collective-permute-start.5 = (bf16[128,512]{1,0:T(8,128)(2,1)S(1)}, bf16[128,512]{1,0:T(8,128)(2,1)S(1)}, u32[]{:S(2)}, u32[]{:S(2)}) collective-permute-start(bf16[128,512]{1,0:T(8,128)(2,1)S(1)} %collective-permute-done.4.one_ref), channel_id=1, source_target_pairs={{0,1},{1,0},{2,3},{3,2},{4,5},{5,4},{6,7},{7,6},{8,9},{9,8},{10,11... | collective-permute-start | bytes 393224 | tf_op jit(solution)/shard_map/ppermute | solution.py:252
  25.1 1.2 %pair.5 = (bf16[10,25,128,128]{3,2,1,0:T(8,128)(2,1)}, bf16[2,25,128,128]{3,2,1,0:T(8,128)(2,1)S(1)}) custom-call(bf16[3200,512]{1,0:T(8,128)(2,1)S(1)} %get-tuple-element.16.shifted_ref, f32[128,128]{1,0:T(8,128)S(1)} %get-tuple-element.17.scale_ref, f32[10,128]{1,0:T(8,128)S(1)} %get-tuple-element.18.weight_ref, ...), custom_call_target="tpu_custom_call" | custom-call | flops 838860800 | bytes 1638400 | tf_op jit(solution)/shard_map/pair/pallas_call | solution.py:232
  26.3 0.0 collective-permute-done.6.one_ref
  26.4 0.0 collective-permute-done.7.two_ref
  26.4 1.3 %pair.6 = (bf16[10,25,128,128]{3,2,1,0:T(8,128)(2,1)}, bf16[2,25,128,128]{3,2,1,0:T(8,128)(2,1)S(1)}) custom-call(bf16[3200,512]{1,0:T(8,128)(2,1)S(1)} %get-tuple-element.16.shifted_ref, f32[128,128]{1,0:T(8,128)S(1)} %get-tuple-element.17.scale_ref, f32[10,128]{1,0:T(8,128)S(1)} %get-tuple-element.18.weight_ref, ...), custom_call_target="tpu_custom_call", output_to_operand_aliasing={{0}: (6, {})} | custom-call | flops 838860800 | bytes 1638400 | tf_op jit(solution)/shard_map/pair/pallas_call | solution.py:232
  27.6 0.0 collective-permute-done.5.two_ref
  27.7 1.3 %pair.7 = (bf16[10,25,128,128]{3,2,1,0:T(8,128)(2,1)}, bf16[2,25,128,128]{3,2,1,0:T(8,128)(2,1)S(1)}) custom-call(bf16[3200,512]{1,0:T(8,128)(2,1)S(1)} %get-tuple-element.16.shifted_ref, f32[128,128]{1,0:T(8,128)S(1)} %get-tuple-element.17.scale_ref, f32[10,128]{1,0:T(8,128)S(1)} %get-tuple-element.18.weight_ref, ...), custom_call_target="tpu_custom_call", output_to_operand_aliasing={{0}: (6, {})} | custom-call | flops 838860800 | bytes 1638400 | tf_op jit(solution)/shard_map/pair/pallas_call | solution.py:232
  28.9 1.3 %pair.8 = (bf16[10,25,128,128]{3,2,1,0:T(8,128)(2,1)}, bf16[2,25,128,128]{3,2,1,0:T(8,128)(2,1)S(1)}) custom-call(bf16[3200,512]{1,0:T(8,128)(2,1)S(1)} %get-tuple-element.16.shifted_ref, f32[128,128]{1,0:T(8,128)S(1)} %get-tuple-element.17.scale_ref, f32[10,128]{1,0:T(8,128)S(1)} %get-tuple-element.18.weight_ref, ...), custom_call_target="tpu_custom_call", output_to_operand_aliasing={{0}: (6, {})} | custom-call | flops 838860800 | bytes 1638400 | tf_op jit(solution)/shard_map/pair/pallas_call | solution.py:232
  30.2 0.0 collective-permute-done.3.one_ref.two_ref
  30.2 2.3 %pair.9 = bf16[10,25,128,128]{3,2,1,0:T(8,128)(2,1)} custom-call(bf16[3200,512]{1,0:T(8,128)(2,1)S(1)} %get-tuple-element.16.shifted_ref, f32[128,128]{1,0:T(8,128)S(1)} %get-tuple-element.17.scale_ref, f32[10,128]{1,0:T(8,128)S(1)} %get-tuple-element.18.weight_ref, ...), custom_call_target="tpu_custom_call", output_to_operand_aliasing={{}: (6, {})} | custom-call | flops 838860800 | bytes 1638400 | tf_op jit(solution)/shard_map/pair/pallas_call | solution.py:232
  (2 shorter events, 0.1 us)
Async XLA Ops:
  1.9 11.1 %collective-permute-start = (bf16[128,512]{1,0:T(8,128)(2,1)S(1)}, bf16[128,512]{1,0:T(8,128)(2,1)S(1)}, u32[]{:S(2)}, u32[]{:S(2)}) collective-permute-start(bf16[128,512]{1,0:T(8,128)(2,1)S(1)} %filter_rows.1.own_ref.one_ref), channel_id=1, source_target_pairs={{0,248},{1,249},{2,250},{3,251},{4,252},{5,253},{6,254},{7,255},{8... | collective-permute-start | bytes 393224 | tf_op jit(solution)/shard_map/ppermute | solution.py:252
  13.0 9.7 %collective-permute-start.1 = (bf16[128,512]{1,0:T(8,128)(2,1)S(1)}, bf16[128,512]{1,0:T(8,128)(2,1)S(1)}, u32[]{:S(2)}, u32[]{:S(2)}) collective-permute-start(bf16[128,512]{1,0:T(8,128)(2,1)S(1)} %get-tuple-element.29), channel_id=1, source_target_pairs={{0,6},{1,7},{2,4},{3,5},{4,2},{5,3},{6,0},{7,1},{8,14},{9,15},{10,... | collective-permute-start | bytes 393224 | tf_op jit(solution)/shard_map/ppermute | solution.py:252
  15.6 7.1 %collective-permute-start.2 = (bf16[128,512]{1,0:T(8,128)(2,1)S(1)}, bf16[128,512]{1,0:T(8,128)(2,1)S(1)}, u32[]{:S(2)}, u32[]{:S(2)}) collective-permute-start(bf16[128,512]{1,0:T(8,128)(2,1)S(1)} %get-tuple-element.28), channel_id=1, source_target_pairs={{0,4},{1,5},{2,6},{3,7},{4,0},{5,1},{6,2},{7,3},{8,12},{9,13},{10,... | collective-permute-start | bytes 393224 | tf_op jit(solution)/shard_map/ppermute | solution.py:252
  16.1 8.5 %collective-permute-start.4 = (bf16[128,512]{1,0:T(8,128)(2,1)S(1)}, bf16[128,512]{1,0:T(8,128)(2,1)S(1)}, u32[]{:S(2)}, u32[]{:S(2)}) collective-permute-start(bf16[128,512]{1,0:T(8,128)(2,1)S(1)} %get-tuple-element.27), channel_id=1, source_target_pairs={{0,2},{1,3},{2,0},{3,1},{4,6},{5,7},{6,4},{7,5},{8,10},{9,11},{10,... | collective-permute-start | bytes 393224 | tf_op jit(solution)/shard_map/ppermute | solution.py:252
  16.4 10.0 %collective-permute-start.6 = (bf16[128,512]{1,0:T(8,128)(2,1)S(1)}, bf16[128,512]{1,0:T(8,128)(2,1)S(1)}, u32[]{:S(2)}, u32[]{:S(2)}) collective-permute-start(bf16[128,512]{1,0:T(8,128)(2,1)S(1)} %filter_rows.1.own_ref.one_ref), channel_id=1, source_target_pairs={{0,247},{1,0},{2,249},{3,2},{4,251},{5,4},{6,253},{7,6},{8,255},{9... | collective-permute-start | bytes 393224 | tf_op jit(solution)/shard_map/ppermute | solution.py:252
  19.8 6.6 %collective-permute-start.7 = (bf16[128,512]{1,0:T(8,128)(2,1)S(1)}, bf16[128,512]{1,0:T(8,128)(2,1)S(1)}, u32[]{:S(2)}, u32[]{:S(2)}) collective-permute-start(bf16[128,512]{1,0:T(8,128)(2,1)S(1)} %collective-permute-done.two_ref), channel_id=1, source_target_pairs={{0,1},{1,0},{2,3},{3,2},{4,5},{5,4},{6,7},{7,6},{8,9},{9,8},{10,11... | collective-permute-start | bytes 393224 | tf_op jit(solution)/shard_map/ppermute | solution.py:252
  22.8 7.4 %collective-permute-start.3 = (bf16[2,128,512]{2,1,0:T(8,128)(2,1)S(1)}, bf16[2,128,512]{2,1,0:T(8,128)(2,1)S(1)}, u32[]{:S(2)}, u32[]{:S(2)}) collective-permute-start(bf16[2,128,512]{2,1,0:T(8,128)(2,1)S(1)} %pad_maximum_fusion), channel_id=1, source_target_pairs={{0,1},{1,0},{2,3},{3,2},{4,5},{5,4},{6,7},{7,6},{8,9},{9,8},{10,11... | collective-permute-start | bytes 786440 | tf_op jit(solution)/shard_map/ppermute | solution.py:252
  24.6 3.0 %collective-permute-start.5 = (bf16[128,512]{1,0:T(8,128)(2,1)S(1)}, bf16[128,512]{1,0:T(8,128)(2,1)S(1)}, u32[]{:S(2)}, u32[]{:S(2)}) collective-permute-start(bf16[128,512]{1,0:T(8,128)(2,1)S(1)} %collective-permute-done.4.one_ref), channel_id=1, source_target_pairs={{0,1},{1,0},{2,3},{3,2},{4,5},{5,4},{6,7},{7,6},{8,9},{9,8},{10,11... | collective-permute-start | bytes 393224 | tf_op jit(solution)/shard_map/ppermute | solution.py:252

commit v3 on v2

--- a/solution.py
+++ b/solution.py
@@ -275,13 +275,12 @@
     x1 = ahead(1)
     x3 = ahead(3)
     x2 = ahead(2)
-    above_s = swapped(above)
-    x1_s = swapped(x1)
+    early_s = swapped(jnp.stack([above, x1]))
     two_s = swapped(jnp.stack([x3, x2]))
     none = (None, None)
     carried = correlate_pair(None, (0, 8), (own, above), none, held)
-    carried = correlate_pair(carried, ((1, 9), (9, 7)), (mixed, above_s), none, held)
-    carried = correlate_pair(carried, ((2, 2, 6, 6), (3, 1, 7, 5)), (x1, x1_s), none, held)
+    carried = correlate_pair(carried, ((2, 2, 6, 6), (1, 9)), (x1, mixed), none, held)
+    carried = correlate_pair(carried, ((9, 7), (3, 1, 7, 5)), (early_s, early_s), (0, 1), held)
     carried = correlate_pair(carried, ((6, 6, 2, 2), 4), (x3, x2), none, held)
     parts = ((0, 15), (15, LAGS))
     carried = correlate_pair(carried, ((7, 5, 3, 1), (5, 3)), (two_s, two_s), (0, 1), held, parts, 2)

time: 32.6 us -> 32.7 us (level)
    ppermute x8 -> x7, starting transfers between devices: 19.9 us -> 19.9 us  [permuted(): lax.ppermute(block, 'ev', [(s, target(s) % count) for s in range(count)])]
    ppermute x8 -> x7, waiting for transfers between devices: 2.2 us -> 2.2 us  [permuted(): lax.ppermute(block, 'ev', [(s, target(s) % count) for s in range(count)])]
  transfers between devices with their start and end apart: 8 -> 7, of which waited for: 1 -> 1; matrix products, arithmetic and copies ran while one was open for 0% -> 0% of each run, Pallas kernels for 19% -> 19%
where the time goes in v3:
time: 32.7 us; the launch traced here: 32.6 us
  starting transfers between devices  19.9 us (61%)
  Pallas kernels  9.63 us (29%)
  waiting for transfers between devices  2.2 us (7%)
  between operations  0.75 us (2%)
    ppermute x7, starting transfers between devices, permuted(): lax.ppermute(block, 'ev', [(s, target(s) % count) for s in range(count)])  19.9 us
    pallas_call x5, Pallas kernels, correlate_pair(): pl.pallas_call(functools.partial(pair_kernel, slabs, places, before, part...  7.37 us
    ppermute x7, waiting for transfers between devices, permuted(): lax.ppermute(block, 'ev', [(s, target(s) % count) for s in range(count)])  2.2 us
    pallas_call x1, Pallas kernels, filtered(): pl.pallas_call(filter_kernel, out_shape=jax.ShapeDtypeStruct((events, sam...  1.25 us
    pallas_call x1, Pallas kernels, shifted_rows(): pl.pallas_call(functools.partial(shift_kernel, count), out_shape=(jax.Sha...  1.02 us
  transfers between devices with their start and end apart: 7, of which 1 were waited for; matrix products, arithmetic and copies ran while one was open for 0% of the time, Pallas kernels for 19%

profile of v3, /device:TPU:1, one launch (start us, length us, event | category | flops | bytes accessed | tf_op | source)
XLA Modules:
  0.0 32.6 jit_solution(6305710483312035513)
XLA Ops:
  0.7 1.2 %filter_rows.1.own_ref.one_ref = bf16[128,512]{1,0:T(8,128)(2,1)S(1)} custom-call(s32[1]{0:T(128)S(6)} %copy.13.live_ref, bf16[1,65]{1,0:T(2,128)(2,1)} %bitcast.10, bf16[128,512]{1,0:T(8,128)(2,1)} %records_hbm.1), custom_call_target="tpu_custom_call" | custom-call | tf_op jit(solution)/shard_map/filter_rows/pallas_call | solution.py:75
  1.9 8.9 %collective-permute-start = (bf16[128,512]{1,0:T(8,128)(2,1)S(1)}, bf16[128,512]{1,0:T(8,128)(2,1)S(1)}, u32[]{:S(2)}, u32[]{:S(2)}) collective-permute-start(bf16[128,512]{1,0:T(8,128)(2,1)S(1)} %filter_rows.1.own_ref.one_ref), channel_id=1, source_target_pairs={{0,248},{1,249},{2,250},{3,251},{4,252},{5,253},{6,254},{7,255},{8... | collective-permute-start | bytes 393224 | tf_op jit(solution)/shard_map/ppermute | solution.py:252
  10.8 2.2 %collective-permute-done.two_ref = bf16[128,512]{1,0:T(8,128)(2,1)S(1)} collective-permute-done((bf16[128,512]{1,0:T(8,128)(2,1)S(1)}, bf16[128,512]{1,0:T(8,128)(2,1)S(1)}, u32[]{:S(2)}, u32[]{:S(2)}) %collective-permute-start) | collective-permute-done | bytes 131104 | tf_op jit(solution)/shard_map/ppermute | solution.py:252
  13.0 1.3 %collective-permute-start.4 = (bf16[128,512]{1,0:T(8,128)(2,1)S(1)}, bf16[128,512]{1,0:T(8,128)(2,1)S(1)}, u32[]{:S(2)}, u32[]{:S(2)}) collective-permute-start(bf16[128,512]{1,0:T(8,128)(2,1)S(1)} %get-tuple-element.27), channel_id=1, source_target_pairs={{0,2},{1,3},{2,0},{3,1},{4,6},{5,7},{6,4},{7,5},{8,10},{9,11},{10,... | collective-permute-start | bytes 393224 | tf_op jit(solution)/shard_map/ppermute | solution.py:252
  14.3 1.8 %collective-permute-start.1 = (bf16[128,512]{1,0:T(8,128)(2,1)S(1)}, bf16[128,512]{1,0:T(8,128)(2,1)S(1)}, u32[]{:S(2)}, u32[]{:S(2)}) collective-permute-start(bf16[128,512]{1,0:T(8,128)(2,1)S(1)} %get-tuple-element.29), channel_id=1, source_target_pairs={{0,6},{1,7},{2,4},{3,5},{4,2},{5,3},{6,0},{7,1},{8,14},{9,15},{10,... | collective-permute-start | bytes 393224 | tf_op jit(solution)/shard_map/ppermute | solution.py:252
  16.2 0.6 %collective-permute-start.2 = (bf16[128,512]{1,0:T(8,128)(2,1)S(1)}, bf16[128,512]{1,0:T(8,128)(2,1)S(1)}, u32[]{:S(2)}, u32[]{:S(2)}) collective-permute-start(bf16[128,512]{1,0:T(8,128)(2,1)S(1)} %get-tuple-element.28), channel_id=1, source_target_pairs={{0,4},{1,5},{2,6},{3,7},{4,0},{5,1},{6,2},{7,3},{8,12},{9,13},{10,... | collective-permute-start | bytes 393224 | tf_op jit(solution)/shard_map/ppermute | solution.py:252
  16.8 2.1 %collective-permute-start.6 = (bf16[128,512]{1,0:T(8,128)(2,1)S(1)}, bf16[128,512]{1,0:T(8,128)(2,1)S(1)}, u32[]{:S(2)}, u32[]{:S(2)}) collective-permute-start(bf16[128,512]{1,0:T(8,128)(2,1)S(1)} %filter_rows.1.own_ref.one_ref), channel_id=1, source_target_pairs={{0,247},{1,0},{2,249},{3,2},{4,251},{5,4},{6,253},{7,6},{8,255},{9... | collective-permute-start | bytes 393224 | tf_op jit(solution)/shard_map/ppermute | solution.py:252
  18.9 1.0 %shift_rows.1 = (bf16[3200,512]{1,0:T(8,128)(2,1)S(1)}, f32[128,128]{1,0:T(8,128)S(1)}, f32[10,128]{1,0:T(8,128)S(1)}) custom-call(s32[1,9]{1,0:T(1,128)} %valid_hbm.1, bf16[128,512]{1,0:T(8,128)(2,1)S(1)} %filter_rows.1.own_ref.one_ref), custom_call_target="tpu_custom_call" | custom-call | bytes 3145728 | tf_op jit(solution)/shard_map/shift_rows/pallas_call | solution.py:115
  19.9 0.0 collective-permute-done.4.one_ref
  20.0 2.8 %collective-permute-start.5 = (bf16[2,128,512]{2,1,0:T(8,128)(2,1)S(1)}, bf16[2,128,512]{2,1,0:T(8,128)(2,1)S(1)}, u32[]{:S(2)}, u32[]{:S(2)}) collective-permute-start(bf16[2,128,512]{2,1,0:T(8,128)(2,1)S(1)} %pad_maximum_fusion.1), channel_id=1, source_target_pairs={{0,1},{1,0},{2,3},{3,2},{4,5},{5,4},{6,7},{7,6},{8,9},{9,8},{10,11... | collective-permute-start | bytes 786440 | tf_op jit(solution)/shard_map/ppermute | solution.py:252
  22.8 0.0 collective-permute-done.1.one_ref
  22.8 0.0 collective-permute-done.2.two_ref
  22.8 2.4 %collective-permute-start.3 = (bf16[2,128,512]{2,1,0:T(8,128)(2,1)S(1)}, bf16[2,128,512]{2,1,0:T(8,128)(2,1)S(1)}, u32[]{:S(2)}, u32[]{:S(2)}) collective-permute-start(bf16[2,128,512]{2,1,0:T(8,128)(2,1)S(1)} %pad_maximum_fusion), channel_id=1, source_target_pairs={{0,1},{1,0},{2,3},{3,2},{4,5},{5,4},{6,7},{7,6},{8,9},{9,8},{10,11... | collective-permute-start | bytes 786440 | tf_op jit(solution)/shard_map/ppermute | solution.py:252
  25.2 1.2 %pair.5 = (bf16[10,25,128,128]{3,2,1,0:T(8,128)(2,1)}, bf16[2,25,128,128]{3,2,1,0:T(8,128)(2,1)S(1)}) custom-call(bf16[3200,512]{1,0:T(8,128)(2,1)S(1)} %get-tuple-element.16.shifted_ref, f32[128,128]{1,0:T(8,128)S(1)} %get-tuple-element.17.scale_ref, f32[10,128]{1,0:T(8,128)S(1)} %get-tuple-element.18.weight_ref, ...), custom_call_target="tpu_custom_call" | custom-call | flops 838860800 | bytes 1638400 | tf_op jit(solution)/shard_map/pair/pallas_call | solution.py:232
  26.4 0.0 collective-permute-done.6.two_ref
  26.4 1.3 %pair.6 = (bf16[10,25,128,128]{3,2,1,0:T(8,128)(2,1)}, bf16[2,25,128,128]{3,2,1,0:T(8,128)(2,1)S(1)}) custom-call(bf16[3200,512]{1,0:T(8,128)(2,1)S(1)} %get-tuple-element.16.shifted_ref, f32[128,128]{1,0:T(8,128)S(1)} %get-tuple-element.17.scale_ref, f32[10,128]{1,0:T(8,128)S(1)} %get-tuple-element.18.weight_ref, ...), custom_call_target="tpu_custom_call", output_to_operand_aliasing={{0}: (6, {})} | custom-call | flops 838860800 | bytes 1638400 | tf_op jit(solution)/shard_map/pair/pallas_call | solution.py:232
  27.7 0.0 collective-permute-done.5.one_ref.two_ref
  27.7 1.3 %pair.7 = (bf16[10,25,128,128]{3,2,1,0:T(8,128)(2,1)}, bf16[2,25,128,128]{3,2,1,0:T(8,128)(2,1)S(1)}) custom-call(bf16[3200,512]{1,0:T(8,128)(2,1)S(1)} %get-tuple-element.16.shifted_ref, f32[128,128]{1,0:T(8,128)S(1)} %get-tuple-element.17.scale_ref, f32[10,128]{1,0:T(8,128)S(1)} %get-tuple-element.18.weight_ref, ...), custom_call_target="tpu_custom_call", output_to_operand_aliasing={{0}: (6, {})} | custom-call | flops 838860800 | bytes 1638400 | tf_op jit(solution)/shard_map/pair/pallas_call | solution.py:232
  29.0 1.3 %pair.8 = (bf16[10,25,128,128]{3,2,1,0:T(8,128)(2,1)}, bf16[2,25,128,128]{3,2,1,0:T(8,128)(2,1)S(1)}) custom-call(bf16[3200,512]{1,0:T(8,128)(2,1)S(1)} %get-tuple-element.16.shifted_ref, f32[128,128]{1,0:T(8,128)S(1)} %get-tuple-element.17.scale_ref, f32[10,128]{1,0:T(8,128)S(1)} %get-tuple-element.18.weight_ref, ...), custom_call_target="tpu_custom_call", output_to_operand_aliasing={{0}: (6, {})} | custom-call | flops 838860800 | bytes 1638400 | tf_op jit(solution)/shard_map/pair/pallas_call | solution.py:232
  30.3 0.0 collective-permute-done.3.one_ref.two_ref
  30.3 2.3 %pair.9 = bf16[10,25,128,128]{3,2,1,0:T(8,128)(2,1)} custom-call(bf16[3200,512]{1,0:T(8,128)(2,1)S(1)} %get-tuple-element.16.shifted_ref, f32[128,128]{1,0:T(8,128)S(1)} %get-tuple-element.17.scale_ref, f32[10,128]{1,0:T(8,128)S(1)} %get-tuple-element.18.weight_ref, ...), custom_call_target="tpu_custom_call", output_to_operand_aliasing={{}: (6, {})} | custom-call | flops 838860800 | bytes 1638400 | tf_op jit(solution)/shard_map/pair/pallas_call | solution.py:232
  (3 shorter events, 0.1 us)
Async XLA Ops:
  1.9 11.1 %collective-permute-start = (bf16[128,512]{1,0:T(8,128)(2,1)S(1)}, bf16[128,512]{1,0:T(8,128)(2,1)S(1)}, u32[]{:S(2)}, u32[]{:S(2)}) collective-permute-start(bf16[128,512]{1,0:T(8,128)(2,1)S(1)} %filter_rows.1.own_ref.one_ref), channel_id=1, source_target_pairs={{0,248},{1,249},{2,250},{3,251},{4,252},{5,253},{6,254},{7,255},{8... | collective-permute-start | bytes 393224 | tf_op jit(solution)/shard_map/ppermute | solution.py:252
  13.0 6.9 %collective-permute-start.4 = (bf16[128,512]{1,0:T(8,128)(2,1)S(1)}, bf16[128,512]{1,0:T(8,128)(2,1)S(1)}, u32[]{:S(2)}, u32[]{:S(2)}) collective-permute-start(bf16[128,512]{1,0:T(8,128)(2,1)S(1)} %get-tuple-element.27), channel_id=1, source_target_pairs={{0,2},{1,3},{2,0},{3,1},{4,6},{5,7},{6,4},{7,5},{8,10},{9,11},{10,... | collective-permute-start | bytes 393224 | tf_op jit(solution)/shard_map/ppermute | solution.py:252
  14.3 8.4 %collective-permute-start.1 = (bf16[128,512]{1,0:T(8,128)(2,1)S(1)}, bf16[128,512]{1,0:T(8,128)(2,1)S(1)}, u32[]{:S(2)}, u32[]{:S(2)}) collective-permute-start(bf16[128,512]{1,0:T(8,128)(2,1)S(1)} %get-tuple-element.29), channel_id=1, source_target_pairs={{0,6},{1,7},{2,4},{3,5},{4,2},{5,3},{6,0},{7,1},{8,14},{9,15},{10,... | collective-permute-start | bytes 393224 | tf_op jit(solution)/shard_map/ppermute | solution.py:252
  16.2 6.6 %collective-permute-start.2 = (bf16[128,512]{1,0:T(8,128)(2,1)S(1)}, bf16[128,512]{1,0:T(8,128)(2,1)S(1)}, u32[]{:S(2)}, u32[]{:S(2)}) collective-permute-start(bf16[128,512]{1,0:T(8,128)(2,1)S(1)} %get-tuple-element.28), channel_id=1, source_target_pairs={{0,4},{1,5},{2,6},{3,7},{4,0},{5,1},{6,2},{7,3},{8,12},{9,13},{10,... | collective-permute-start | bytes 393224 | tf_op jit(solution)/shard_map/ppermute | solution.py:252
  16.8 9.6 %collective-permute-start.6 = (bf16[128,512]{1,0:T(8,128)(2,1)S(1)}, bf16[128,512]{1,0:T(8,128)(2,1)S(1)}, u32[]{:S(2)}, u32[]{:S(2)}) collective-permute-start(bf16[128,512]{1,0:T(8,128)(2,1)S(1)} %filter_rows.1.own_ref.one_ref), channel_id=1, source_target_pairs={{0,247},{1,0},{2,249},{3,2},{4,251},{5,4},{6,253},{7,6},{8,255},{9... | collective-permute-start | bytes 393224 | tf_op jit(solution)/shard_map/ppermute | solution.py:252
  20.0 7.8 %collective-permute-start.5 = (bf16[2,128,512]{2,1,0:T(8,128)(2,1)S(1)}, bf16[2,128,512]{2,1,0:T(8,128)(2,1)S(1)}, u32[]{:S(2)}, u32[]{:S(2)}) collective-permute-start(bf16[2,128,512]{2,1,0:T(8,128)(2,1)S(1)} %pad_maximum_fusion.1), channel_id=1, source_target_pairs={{0,1},{1,0},{2,3},{3,2},{4,5},{5,4},{6,7},{7,6},{8,9},{9,8},{10,11... | collective-permute-start | bytes 786440 | tf_op jit(solution)/shard_map/ppermute | solution.py:252
  22.8 7.5 %collective-permute-start.3 = (bf16[2,128,512]{2,1,0:T(8,128)(2,1)S(1)}, bf16[2,128,512]{2,1,0:T(8,128)(2,1)S(1)}, u32[]{:S(2)}, u32[]{:S(2)}) collective-permute-start(bf16[2,128,512]{2,1,0:T(8,128)(2,1)S(1)} %pad_maximum_fusion), channel_id=1, source_target_pairs={{0,1},{1,0},{2,3},{3,2},{4,5},{5,4},{6,7},{7,6},{8,9},{9,8},{10,11... | collective-permute-start | bytes 786440 | tf_op jit(solution)/shard_map/ppermute | solution.py:252
